TPU v7x, 32 devices: a whole 2x2x4 slice. The times are simulated.
32 devices in a mesh: segment: 2 (over x), rows: 8 (over z, y), cols: 2 (over core).
Axes of the slice: x: 2, y: 2, z: 4, core: 2. Of those that a mesh axis runs over, the one named last changes fastest.
Arguments:
- frames: bfloat16 [2, 2, 16, 128, 128], P(None, None, 'rows', 'cols'), may hold values from -6 to 6
- cell_weight: bfloat16 [9, 256, 512], P(None, 'rows'), may hold values from -0.125 to 0.125
- cell_bias: float32 [512], replicated, may hold values from -3 to 3
- first_context_weight: bfloat16 [9, 128, 384], P(None, 'rows'), may hold values from -1 to 1
- first_context_bias: float32 [384], replicated, may hold values from -0.5 to 1
- second_context_weight: bfloat16 [9, 384, 384], P(None, 'rows'), may hold values from -0.109375 to 0.109375
- second_context_bias: float32 [384], replicated, may hold values from -0.5 to 1
- third_context_weight: bfloat16 [9, 384, 384], P(None, 'rows'), may hold values from -0.109375 to 0.109375
- third_context_bias: float32 [384], replicated, may hold values from 0 to 1
Outputs:
- context: bfloat16 [2, 16, 128, 384], P('segment', 'rows', 'cols')
All inputs are finite; a program needn't handle non-finite values.
Results may differ from a plain program's by a relative error of at most 0.0065.
Values may be sent and summed in bfloat16 or wider, within the bound.
A program may use at most 64 MiB of HBM per device.

v0:
```python
import jax
import jax.numpy as jnp
from jax import lax
from jax.sharding import PartitionSpec as P

FIRST_DILATION = 16
SECOND_DILATION = 32
THIRD_DILATION = 64


def extended(value, sides, width):
    for axis, dim in sides:
        devices, length = (lax.axis_size(axis), value.shape[dim])
        up = [(i, (i + 1) % devices) for i in range(devices - 1)]
        down = [(j, i) for i, j in up]
        last = lax.slice_in_dim(value, length - width, length, axis=dim)
        leading = lax.slice_in_dim(value, 0, width, axis=dim)
        before = lax.ppermute(last, axis, up)
        after = lax.ppermute(leading, axis, down)
        value = jnp.concatenate([before, value, after], axis=dim)
    return value


def shortened(value):

    def short(part):
        return part.astype(jnp.bfloat16) if part.dtype == jnp.float32 else part

    return jax.tree.map(short, value)


def from_behind(value, axis, steps):
    count = lax.axis_size(axis)
    leading, last = (max(0, -steps), min(count, count - steps))
    return lax.ppermute(value, axis, [(source, source + steps) for source in range(leading, last)])


def tap_product(tap_list, weight):
    stacked = jnp.concatenate(tap_list, axis=-1)
    height, across, channels = stacked.shape
    flattened = stacked.reshape(height * across, channels)
    product = jnp.dot(
        flattened, weight.reshape(channels, weight.shape[-1]), preferred_element_type=jnp.float32
    )
    return product.reshape(height, across, weight.shape[-1])


def cell_update(padded, memory, weight, offset):
    height, across, channels = memory.shape
    tap_list = [
        padded[row_tap : row_tap + height, col_tap : col_tap + across]
        for row_tap in range(3)
        for col_tap in range(3)
    ]
    gate_sums = tap_product(tap_list, weight) + offset
    inflow = jax.nn.sigmoid(gate_sums[..., :channels])
    forget = jax.nn.sigmoid(gate_sums[..., channels : 2 * channels])
    output = jax.nn.sigmoid(gate_sums[..., 2 * channels : 3 * channels])
    update = jnp.tanh(gate_sums[..., 3 * channels :])
    memory = forget * memory + inflow * update
    hidden_state = (output * jnp.tanh(memory)).astype(jnp.bfloat16)
    return (hidden_state, memory)


def cell_section(clip, weight, offset, active_mask):
    height, across = (clip.shape[1], clip.shape[2])
    channels = offset.shape[0] // 4
    hidden_state = jnp.zeros((height, across, channels), jnp.bfloat16)
    memory = jnp.zeros((height, across, channels), jnp.float32)

    def cell_compute(operands):
        return cell_update(operands[0], operands[1], weight, offset)

    def cell_skipped(operands):
        return (jnp.zeros((height, across, channels), jnp.bfloat16), jnp.zeros_like(operands[1]))

    for moment in range(clip.shape[0]):
        joined = jnp.concatenate([clip[moment], hidden_state], axis=-1)
        padded = extended(joined, (("rows", 0), ("cols", 1)), 1)
        hidden_state, memory = lax.cond(active_mask, cell_compute, cell_skipped, (padded, memory))
    return hidden_state


def dilated_context_layer(feature, weight, offset, spacing, active_mask):
    height, across = (feature.shape[0], feature.shape[1])
    widened = extended(feature, (("cols", 1),), spacing)
    reach = spacing // height
    groups = lax.axis_size("rows")
    if reach >= groups:
        before = jnp.zeros_like(widened)
        beyond = jnp.zeros_like(widened)
    else:
        before = from_behind(shortened(widened), "rows", reach).astype(widened.dtype)
        beyond = from_behind(shortened(widened), "rows", -reach).astype(widened.dtype)
    row_taps = [before, widened, beyond]
    tap_list = [
        row_taps[row_tap][:, col_tap * spacing : col_tap * spacing + across]
        for row_tap in range(3)
        for col_tap in range(3)
    ]

    def dilated_compute(pieces):
        return jnp.maximum(tap_product(pieces, weight) + offset, 0.0)

    def dilated_skipped(pieces):
        return jnp.zeros((height, across, weight.shape[-1]), jnp.float32)

    return lax.cond(active_mask, dilated_compute, dilated_skipped, tap_list)


def context_section(hidden_state, kernel_list, offset_list, active_mask):
    first_output = dilated_context_layer(
        hidden_state, kernel_list[0], offset_list[0], FIRST_DILATION, active_mask
    ).astype(jnp.bfloat16)
    second_output = dilated_context_layer(
        first_output, kernel_list[1], offset_list[1], SECOND_DILATION, active_mask
    ).astype(jnp.bfloat16)
    third_output = dilated_context_layer(
        second_output, kernel_list[2], offset_list[2], THIRD_DILATION, active_mask
    )
    return (second_output.astype(jnp.float32) + third_output).astype(jnp.bfloat16)


def per_device(
    frames,
    cell_weight,
    cell_bias,
    first_context_weight,
    first_context_bias,
    second_context_weight,
    second_context_bias,
    third_context_weight,
    third_context_bias,
):
    full_cell, full_first, full_second, full_third = (
        lax.all_gather(cell_weight, "rows", axis=1, tiled=True),
        lax.all_gather(first_context_weight, "rows", axis=1, tiled=True),
        lax.all_gather(second_context_weight, "rows", axis=1, tiled=True),
        lax.all_gather(third_context_weight, "rows", axis=1, tiled=True),
    )
    kernel_list = (full_first, full_second, full_third)
    offset_list = (first_context_bias, second_context_bias, third_context_bias)
    segment_index = lax.axis_index("segment")
    micro_count = frames.shape[0]
    half_count = micro_count // 2
    always = jnp.array(True)
    own_frames = lax.dynamic_slice_in_dim(frames, segment_index * half_count, half_count, 0)
    state = cell_section(own_frames[0], full_cell, cell_bias, always)
    results = [context_section(state, kernel_list, offset_list, always)]
    return jnp.stack(results)


def solution(mesh):
    placed = (
        P(None, None, "rows", "cols", None),
        P(None, "rows", None),
        P(),
        P(None, "rows", None),
        P(),
        P(None, "rows", None),
        P(),
        P(None, "rows", None),
        P(),
    )
    return jax.shard_map(
        per_device,
        mesh=mesh,
        in_specs=placed,
        out_specs=P("segment", "rows", "cols", None),
        check_vma=False,
    )
```

profile of v0, /device:TPU:0, one launch (start us, length us, event | category | flops | bytes accessed | tf_op | source)
XLA Modules:
  0.0 190.7 jit_solution(9595188403604663498)
XLA Ops:
  6.5 0.7 all-gather.4.cloned.1.call-update
  7.3 0.7 all-gather.6.cloned.1.call-update
  8.1 0.8 dynamic-slice_bitcast_fusion.1
  8.9 4.9 %collective-permute-start = (bf16[1,64,256]{2,1,0:T(8,128)(2,1)S(1)}, bf16[1,64,256]{2,1,0:T(8,128)(2,1)S(1)}, u32[]{:S(2)}, u32[]{:S(2)}) collective-permute-start(bf16[1,64,256]{2,1,0:T(8,128)(2,1)S(1)} %get-tuple-element.23), channel_id=1, source_target_pairs={{0,2},{2,4},{4,6},{6,8},{8,10},{10,12},{12,14},{1,3},{3,5},{5,7},{... | collective-permute-start | bytes 98312 | tf_op jit(solution)/shard_map/ppermute | solution.py:18
  13.8 1.3 collective-permute-start.1
  15.1 36.8 %all_gather.13 = bf16[9,128,384]{2,1,0:T(8,128)(2,1)S(1)} all-gather(bf16[9,16,384]{2,1,0:T(8,128)(2,1)} %param.12), channel_id=1, replica_groups=mesh['segment'=2,'rows'=8,'cols'=2] {'rows'}, dimensions={1}, use_global_device_ids=true | all-gather | bytes 995328 | tf_op jit(solution)/shard_map/all_gather | solution.py:137
  52.0 1.3 collective-permute-start.2
  53.3 1.3 collective-permute-start.3
  54.6 1.7 collective-permute-done.3
  56.6 12.3 %all-gather.4.cloned.1.call-done = bf16[9,256,512]{2,1,0:T(8,128)(2,1)} async-done(((bf16[9,32,512]{2,1,0:T(8,128)(2,1)}), bf16[9,256,512]{2,1,0:T(8,128)(2,1)}) %all-gather.4.cloned.1.call-update) | async-done | bytes 2359312 | tf_op jit(solution)/shard_map/all_gather | solution.py:136
  68.9 2.3 %convolution_add_fusion.1 = f32[2,64,512]{2,1,0:T(8,128)S(1)} fusion(bf16[2,64,2304]{2,1,0:T(8,128)(2,1)S(1)} %constant_dynamic-update-slice_fusion, bf16[2304,512,1]{1,0,2:T(8,128)(2,1)} %bitcast.28, f32[512]{0:T(512)S(1)} %copy-done.1), kind=kOutput, calls=%fused_computation.1 | convolution fusion | flops 302055424 | bytes 3213312 | tf_op jit(solution)/shard_map/cond/branch_1_fun/dot_general | solution.py:42
  71.3 3.4 %collective-permute-start.4 = (bf16[1,64,256]{2,1,0:T(8,128)(2,1)S(1)}, bf16[1,64,256]{2,1,0:T(8,128)(2,1)S(1)}, u32[]{:S(2)}, u32[]{:S(2)}) collective-permute-start(bf16[1,64,256]{2,1,0:T(8,128)(2,1)S(1)} %get-tuple-element.19), channel_id=1, source_target_pairs={{0,2},{2,4},{4,6},{6,8},{8,10},{10,12},{12,14},{1,3},{3,5},{5,7},{... | collective-permute-start | bytes 98312 | tf_op jit(solution)/shard_map/ppermute | solution.py:18
  74.7 1.3 collective-permute-start.5
  76.3 4.2 %collective-permute-done.5 = bf16[1,64,256]{2,1,0:T(8,128)(2,1)S(1)} collective-permute-done((bf16[1,64,256]{2,1,0:T(8,128)(2,1)S(1)}, bf16[1,64,256]{2,1,0:T(8,128)(2,1)S(1)}, u32[]{:S(2)}, u32[]{:S(2)}) %collective-permute-start.5) | collective-permute-done | bytes 32800 | tf_op jit(solution)/shard_map/ppermute | solution.py:19
  80.5 1.3 collective-permute-start.6
  81.8 1.3 collective-permute-start.7
  83.1 1.7 collective-permute-done.7
  85.1 0.5 convolution_add_fusion
  85.7 2.1 %collective-permute-start.8 = (bf16[2,16,128]{2,1,0:T(8,128)(2,1)S(1)}, bf16[2,16,128]{2,1,0:T(8,128)(2,1)S(1)}, u32[]{:S(2)}, u32[]{:S(2)}) collective-permute-start(bf16[2,16,128]{2,1,0:T(8,128)(2,1)S(1)} %get-tuple-element.22), channel_id=1, source_target_pairs={{0,1},{2,3},{4,5},{6,7},{8,9},{10,11},{12,13},{14,15},{16,17},{18,... | collective-permute-start | bytes 24584 | tf_op jit(solution)/shard_map/ppermute | solution.py:18
  87.8 1.3 collective-permute-start.9
  89.2 1.7 collective-permute-done.9
  91.0 0.3 fusion.4
  91.3 2.1 %collective-permute-start.10 = (bf16[2,32,384]{2,1,0:T(8,128)(2,1)S(1)}, bf16[2,32,384]{2,1,0:T(8,128)(2,1)S(1)}, u32[]{:S(2)}, u32[]{:S(2)}) collective-permute-start(bf16[2,32,384]{2,1,0:T(8,128)(2,1)S(1)} %get-tuple-element.18), channel_id=1, source_target_pairs={{0,1},{2,3},{4,5},{6,7},{8,9},{10,11},{12,13},{14,15},{16,17},{18,... | collective-permute-start | bytes 147464 | tf_op jit(solution)/shard_map/ppermute | solution.py:18
  93.4 1.3 collective-permute-start.11
  94.8 1.8 collective-permute-done.11
  96.6 29.0 %all-gather.6.cloned.1.call-done = bf16[9,384,384]{2,1,0:T(8,128)(2,1)} async-done(((bf16[9,48,384]{2,1,0:T(8,128)(2,1)}), bf16[9,384,384]{2,1,0:T(8,128)(2,1)}) %all-gather.6.cloned.1.call-update) | async-done | bytes 2654224 | tf_op jit(solution)/shard_map/all_gather | solution.py:138
  125.5 2.4 %fusion.5 = bf16[2,64,384]{2,1,0:T(8,128)(2,1)S(1)} fusion(bf16[2,64,3456]{2,1,0:T(8,128)(2,1)S(1)} %constant_dynamic-update-slice_fusion.27, bf16[3456,384,1]{1,0,2:T(8,128)(2,1)} %bitcast.30, f32[384]{0:T(512)S(1)} %copy-done.3), kind=kOutput, calls=%fused_computation.10 | convolution fusion | flops 339886080 | bytes 3638784 | tf_op jit(solution)/shard_map/cond/branch_1_fun/dot_general | solution.py:42
  128.0 1.3 collective-permute-start.12
  129.3 1.3 collective-permute-start.13
  130.6 1.8 collective-permute-done.13
  132.5 48.6 %all-gather.8.cloned.1.call-done = bf16[9,384,384]{2,1,0:T(8,128)(2,1)} async-done(((bf16[9,48,384]{2,1,0:T(8,128)(2,1)}), bf16[9,384,384]{2,1,0:T(8,128)(2,1)}) %all-gather.8.cloned.1.call-update) | async-done | bytes 2654224 | tf_op jit(solution)/shard_map/all_gather | solution.py:139
  181.2 3.0 %fusion.7 = bf16[1,2,64,384]{3,2,1,0:T(8,128)(2,1)} fusion(bf16[2,64,3456]{2,1,0:T(8,128)(2,1)S(1)} %constant_dynamic-update-slice_fusion.30, bf16[3456,384,1]{1,0,2:T(8,128)(2,1)} %bitcast.32, bf16[2,64,384]{2,1,0:T(8,128)(2,1)S(1)} %fusion.5, f32[384]{0:T(512)S(1)} %copy-done.2), kind=kOutput, calls=%fused_computation.12 | convolution fusion | flops 339984384 | bytes 3737088 | tf_op jit(solution)/shard_map/cond/branch_1_fun/dot_general | solution.py:42
  (74 shorter events, 1.3 us)
Async XLA Ops:
  6.5 62.3 %copy-start.1 = (f32[512]{0:T(512)S(1)}, f32[512]{0:T(512)}, u32[]{:S(2)}) copy-start(f32[512]{0:T(512)} %param.11) | copy-start | bytes 6148
  6.5 62.3 %all-gather.4.cloned.1.call-start = ((), (), s32[]{:S(2)}) async-start(), calls=%async_computation | async-start | bytes 2654208 | tf_op jit(solution)/shard_map/all_gather | solution.py:136
  7.3 118.3 %all-gather.6.cloned.1.call-start = ((), (), s32[]{:S(2)}) async-start(), calls=%async_computation.1 | async-start | bytes 2985984 | tf_op jit(solution)/shard_map/all_gather | solution.py:138
  8.0 173.2 %all-gather.8.cloned.1.call-start = ((), (), s32[]{:S(2)}) async-start(), calls=%async_computation.2 | async-start | bytes 2985984 | tf_op jit(solution)/shard_map/all_gather | solution.py:139
  8.9 43.1 %collective-permute-start = (bf16[1,64,256]{2,1,0:T(8,128)(2,1)S(1)}, bf16[1,64,256]{2,1,0:T(8,128)(2,1)S(1)}, u32[]{:S(2)}, u32[]{:S(2)}) collective-permute-start(bf16[1,64,256]{2,1,0:T(8,128)(2,1)S(1)} %get-tuple-element.23), channel_id=1, source_target_pairs={{0,2},{2,4},{4,6},{6,8},{8,10},{10,12},{12,14},{1,3},{3,5},{5,7},{... | collective-permute-start | bytes 98312 | tf_op jit(solution)/shard_map/ppermute | solution.py:18
  13.8 38.2 %collective-permute-start.1 = (bf16[1,64,256]{2,1,0:T(8,128)(2,1)S(1)}, bf16[1,64,256]{2,1,0:T(8,128)(2,1)S(1)}, u32[]{:S(2)}, u32[]{:S(2)}) collective-permute-start(bf16[1,64,256]{2,1,0:T(8,128)(2,1)S(1)} %get-tuple-element.24), channel_id=1, source_target_pairs={{2,0},{4,2},{6,4},{8,6},{10,8},{12,10},{14,12},{3,1},{5,3},{7,5},{... | collective-permute-start | bytes 98312 | tf_op jit(solution)/shard_map/ppermute | solution.py:19
  52.0 2.6 %collective-permute-start.2 = (bf16[4,1,256]{2,1,0:T(2,128)(2,1)S(1)}, bf16[4,1,256]{2,1,0:T(2,128)(2,1)S(1)}, u32[]{:S(2)}, u32[]{:S(2)}) collective-permute-start(bf16[4,1,256]{2,1,0:T(2,128)(2,1)S(1)} %get-tuple-element.16), channel_id=1, source_target_pairs={{0,1},{2,3},{4,5},{6,7},{8,9},{10,11},{12,13},{14,15},{16,17},{18,... | collective-permute-start | bytes 6152 | tf_op jit(solution)/shard_map/ppermute | solution.py:18
  53.3 3.1 %collective-permute-start.3 = (bf16[4,1,256]{2,1,0:T(2,128)(2,1)S(1)}, bf16[4,1,256]{2,1,0:T(2,128)(2,1)S(1)}, u32[]{:S(2)}, u32[]{:S(2)}) collective-permute-start(bf16[4,1,256]{2,1,0:T(2,128)(2,1)S(1)} %get-tuple-element.15), channel_id=1, source_target_pairs={{1,0},{3,2},{5,4},{7,6},{9,8},{11,10},{13,12},{15,14},{17,16},{19,... | collective-permute-start | bytes 6152 | tf_op jit(solution)/shard_map/ppermute | solution.py:19
  68.9 16.2 %copy-start = (bf16[9,256,512]{2,1,0:T(8,128)(2,1)S(1)}, bf16[9,256,512]{2,1,0:T(8,128)(2,1)}, u32[]{:S(2)}) copy-start(bf16[9,256,512]{2,1,0:T(8,128)(2,1)} %all-gather.4.cloned.1.call-done) | copy-start | bytes 7077892
  71.3 5.0 %collective-permute-start.4 = (bf16[1,64,256]{2,1,0:T(8,128)(2,1)S(1)}, bf16[1,64,256]{2,1,0:T(8,128)(2,1)S(1)}, u32[]{:S(2)}, u32[]{:S(2)}) collective-permute-start(bf16[1,64,256]{2,1,0:T(8,128)(2,1)S(1)} %get-tuple-element.19), channel_id=1, source_target_pairs={{0,2},{2,4},{4,6},{6,8},{8,10},{10,12},{12,14},{1,3},{3,5},{5,7},{... | collective-permute-start | bytes 98312 | tf_op jit(solution)/shard_map/ppermute | solution.py:18
  74.7 5.8 %collective-permute-start.5 = (bf16[1,64,256]{2,1,0:T(8,128)(2,1)S(1)}, bf16[1,64,256]{2,1,0:T(8,128)(2,1)S(1)}, u32[]{:S(2)}, u32[]{:S(2)}) collective-permute-start(bf16[1,64,256]{2,1,0:T(8,128)(2,1)S(1)} %get-tuple-element.20), channel_id=1, source_target_pairs={{2,0},{4,2},{6,4},{8,6},{10,8},{12,10},{14,12},{3,1},{5,3},{7,5},{... | collective-permute-start | bytes 98312 | tf_op jit(solution)/shard_map/ppermute | solution.py:19
  80.5 2.6 %collective-permute-start.6 = (bf16[4,1,256]{2,1,0:T(2,128)(2,1)S(1)}, bf16[4,1,256]{2,1,0:T(2,128)(2,1)S(1)}, u32[]{:S(2)}, u32[]{:S(2)}) collective-permute-start(bf16[4,1,256]{2,1,0:T(2,128)(2,1)S(1)} %get-tuple-element.10), channel_id=1, source_target_pairs={{0,1},{2,3},{4,5},{6,7},{8,9},{10,11},{12,13},{14,15},{16,17},{18,... | collective-permute-start | bytes 6152 | tf_op jit(solution)/shard_map/ppermute | solution.py:18
  81.8 3.1 %collective-permute-start.7 = (bf16[4,1,256]{2,1,0:T(2,128)(2,1)S(1)}, bf16[4,1,256]{2,1,0:T(2,128)(2,1)S(1)}, u32[]{:S(2)}, u32[]{:S(2)}) collective-permute-start(bf16[4,1,256]{2,1,0:T(2,128)(2,1)S(1)} %get-tuple-element.9), channel_id=1, source_target_pairs={{1,0},{3,2},{5,4},{7,6},{9,8},{11,10},{13,12},{15,14},{17,16},{19,... | collective-permute-start | bytes 6152 | tf_op jit(solution)/shard_map/ppermute | solution.py:19
  84.9 6.0 %copy-start.4 = (f32[384]{0:T(512)S(1)}, f32[384]{0:T(512)}, u32[]{:S(2)}) copy-start(f32[384]{0:T(512)} %param.13) | copy-start | bytes 4612
  85.1 40.4 %copy-start.3 = (f32[384]{0:T(512)S(1)}, f32[384]{0:T(512)}, u32[]{:S(2)}) copy-start(f32[384]{0:T(512)} %param.15) | copy-start | bytes 4612
  85.7 3.4 %collective-permute-start.8 = (bf16[2,16,128]{2,1,0:T(8,128)(2,1)S(1)}, bf16[2,16,128]{2,1,0:T(8,128)(2,1)S(1)}, u32[]{:S(2)}, u32[]{:S(2)}) collective-permute-start(bf16[2,16,128]{2,1,0:T(8,128)(2,1)S(1)} %get-tuple-element.22), channel_id=1, source_target_pairs={{0,1},{2,3},{4,5},{6,7},{8,9},{10,11},{12,13},{14,15},{16,17},{18,... | collective-permute-start | bytes 24584 | tf_op jit(solution)/shard_map/ppermute | solution.py:18
  87.8 3.1 %collective-permute-start.9 = (bf16[2,16,128]{2,1,0:T(8,128)(2,1)S(1)}, bf16[2,16,128]{2,1,0:T(8,128)(2,1)S(1)}, u32[]{:S(2)}, u32[]{:S(2)}) collective-permute-start(bf16[2,16,128]{2,1,0:T(8,128)(2,1)S(1)} %get-tuple-element.21), channel_id=1, source_target_pairs={{1,0},{3,2},{5,4},{7,6},{9,8},{11,10},{13,12},{15,14},{17,16},{19,... | collective-permute-start | bytes 24584 | tf_op jit(solution)/shard_map/ppermute | solution.py:19
  91.3 3.4 %collective-permute-start.10 = (bf16[2,32,384]{2,1,0:T(8,128)(2,1)S(1)}, bf16[2,32,384]{2,1,0:T(8,128)(2,1)S(1)}, u32[]{:S(2)}, u32[]{:S(2)}) collective-permute-start(bf16[2,32,384]{2,1,0:T(8,128)(2,1)S(1)} %get-tuple-element.18), channel_id=1, source_target_pairs={{0,1},{2,3},{4,5},{6,7},{8,9},{10,11},{12,13},{14,15},{16,17},{18,... | collective-permute-start | bytes 147464 | tf_op jit(solution)/shard_map/ppermute | solution.py:18
  93.4 3.1 %collective-permute-start.11 = (bf16[2,32,384]{2,1,0:T(8,128)(2,1)S(1)}, bf16[2,32,384]{2,1,0:T(8,128)(2,1)S(1)}, u32[]{:S(2)}, u32[]{:S(2)}) collective-permute-start(bf16[2,32,384]{2,1,0:T(8,128)(2,1)S(1)} %get-tuple-element.17), channel_id=1, source_target_pairs={{1,0},{3,2},{5,4},{7,6},{9,8},{11,10},{13,12},{15,14},{17,16},{19,... | collective-permute-start | bytes 147464 | tf_op jit(solution)/shard_map/ppermute | solution.py:19
  125.5 55.6 %copy-start.2 = (f32[384]{0:T(512)S(1)}, f32[384]{0:T(512)}, u32[]{:S(2)}) copy-start(f32[384]{0:T(512)} %param.17) | copy-start | bytes 4612
  128.0 2.6 %collective-permute-start.12 = (bf16[2,64,384]{2,1,0:T(8,128)(2,1)S(1)}, bf16[2,64,384]{2,1,0:T(8,128)(2,1)S(1)}, u32[]{:S(2)}, u32[]{:S(2)}) collective-permute-start(bf16[2,64,384]{2,1,0:T(8,128)(2,1)S(1)} %fusion.5), channel_id=1, source_target_pairs={{0,1},{2,3},{4,5},{6,7},{8,9},{10,11},{12,13},{14,15},{16,17},{18,... | collective-permute-start | bytes 294920 | tf_op jit(solution)/shard_map/ppermute | solution.py:18
  129.3 3.2 %collective-permute-start.13 = (bf16[2,64,384]{2,1,0:T(8,128)(2,1)S(1)}, bf16[2,64,384]{2,1,0:T(8,128)(2,1)S(1)}, u32[]{:S(2)}, u32[]{:S(2)}) collective-permute-start(bf16[2,64,384]{2,1,0:T(8,128)(2,1)S(1)} %fusion.5), channel_id=1, source_target_pairs={{1,0},{3,2},{5,4},{7,6},{9,8},{11,10},{13,12},{15,14},{17,16},{19,... | collective-permute-start | bytes 294920 | tf_op jit(solution)/shard_map/ppermute | solution.py:19
Sparse Core Ops, SparseCore 0:
  9.5 59.3 all-gather.3
  71.1 54.3 all-gather.5
  127.8 53.3 all-gather.7
where the time goes:
time: 191 us
  waiting for transfers between devices  105 us (55%)
  blocking collectives  36.8 us (19%)
  starting transfers between devices  25.4 us (13%)
  between operations  13.7 us (7%)
  matrix products  8.51 us (4%)
    all_gather x1, waiting for transfers between devices, per_device(): lax.all_gather(third_context_weight, 'rows', axis=1, tiled=True)  48.6 us
    all_gather x1, blocking collectives, per_device(): lax.all_gather(first_context_weight, 'rows', axis=1, tiled=True)  36.8 us
    all_gather x1, waiting for transfers between devices, per_device(): lax.all_gather(second_context_weight, 'rows', axis=1, tiled=True)  29 us
    ppermute x7, starting transfers between devices, extended(): before = lax.ppermute(last, axis, up)  16.3 us
    ppermute x7, waiting for transfers between devices, extended(): after = lax.ppermute(leading, axis, down)  13 us
    all_gather x1, waiting for transfers between devices, per_device(): lax.all_gather(cell_weight, 'rows', axis=1, tiled=True)  12.3 us
    ppermute x7, starting transfers between devices, extended(): after = lax.ppermute(leading, axis, down)  9.04 us
    dot_general x5, matrix products, tap_product(): jnp.dot(flattened, weight.reshape(channels, weight.shape[-1]), preferred_...  8.51 us
  transfers between devices with their start and end apart: 17, of which 10 were waited for; matrix products, arithmetic and copies ran while one was open for 4% of the time, Pallas kernels for 0%

commit v1 on v0

--- a/solution.py
+++ b/solution.py
@@ -6,6 +6,28 @@
 FIRST_DILATION = 16
 SECOND_DILATION = 32
 THIRD_DILATION = 64
+
+
+def in_order(blocks, dim):
+    blocks = jnp.moveaxis(blocks, 0, dim)
+    shape = blocks.shape
+    return blocks.reshape(*shape[:dim], shape[dim] * shape[dim + 1], *shape[dim + 2 :])
+
+
+def collect(shard, axis, dim):
+    size = lax.axis_size(axis)
+    pairs = [(i, (i + 1) % size) for i in range(size)]
+    back = [(b, a) for a, b in pairs]
+    lower, upper = ([], [])
+    for step in range(size - 1):
+        if step % 2 == 0:
+            lower.append(lax.ppermute(lower[-1] if lower else shard, axis, pairs))
+        else:
+            upper.append(lax.ppermute(upper[-1] if upper else shard, axis, back))
+    tiles = jnp.stack([*lower[::-1], shard, *upper])
+    shift = lax.axis_index(axis) - len(lower)
+    tiles = tiles[(jnp.arange(size) - shift) % size]
+    return in_order(tiles, dim)
 
 
 def extended(value, sides, width):
@@ -135,7 +157,7 @@
     full_cell, full_first, full_second, full_third = (
         lax.all_gather(cell_weight, "rows", axis=1, tiled=True),
         lax.all_gather(first_context_weight, "rows", axis=1, tiled=True),
-        lax.all_gather(second_context_weight, "rows", axis=1, tiled=True),
+        collect(second_context_weight, "rows", 1),
         lax.all_gather(third_context_weight, "rows", axis=1, tiled=True),
     )
     kernel_list = (full_first, full_second, full_third)

time: 191 us -> 176 us (0.921)
  waiting for transfers between devices: 105 us -> 53.3 us
  starting transfers between devices: 25.4 us -> 40.7 us
  local copies, waits for them, and re-layouts: 1.32 us -> 16.4 us
  blocking collectives: 36.8 us -> 42.9 us
    all_gather x1, waiting for transfers between devices: 48.6 us -> 0.02 us  [per_device(): lax.all_gather(third_context_weight, 'rows', axis=1, tiled=True)]
    ppermute x0 -> x7, waiting for transfers between devices: none -> 41.8 us  [the longest x4 41.8 us: collect(): lower.append(lax.ppermute(lower[-1] if lower else shard, axis, pairs))]
    all_gather x1 -> x0, waiting for transfers between devices: 29 us -> none  [per_device(): lax.all_gather(second_context_weight, 'rows', axis=1, tiled=True)]
    ppermute x0 -> x7, starting transfers between devices: none -> 16.3 us  [the longest x3 10.2 us: collect(): upper.append(lax.ppermute(upper[-1] if upper else shard, axis, back))]
    all_gather x1, waiting for transfers between devices: 12.3 us -> 0.01 us  [per_device(): lax.all_gather(cell_weight, 'rows', axis=1, tiled=True)]
    unnamed x38 -> x57, local copies, waits for them, and re-layouts: 0.41 us -> 9.92 us
    all_gather x1, blocking collectives: 36.8 us -> 42.9 us  [per_device(): lax.all_gather(first_context_weight, 'rows', axis=1, tiled=True)]
    gather x0 -> x1, local copies, waits for them, and re-layouts: none -> 2.88 us  [collect(): tiles = tiles[(jnp.arange(size) - shift) % size]]
  transfers between devices with their start and end apart: 17 -> 23, of which waited for: 10 -> 9; matrix products, arithmetic and copies ran while one was open for 4% -> 12% of each run, Pallas kernels for 0% -> 0%
where the time goes in v1:
time: 176 us; the launch traced here: 175 us
  waiting for transfers between devices  53.3 us (30%)
  blocking collectives  42.9 us (24%)
  starting transfers between devices  40.7 us (23%)
  local copies, waits for them, and re-layouts  16.4 us (9%)
  between operations  14.1 us (8%)
  matrix products  6.75 us (4%)
    all_gather x1, blocking collectives, per_device(): lax.all_gather(first_context_weight, 'rows', axis=1, tiled=True)  42.9 us
    ppermute x4, waiting for transfers between devices, collect(): lower.append(lax.ppermute(lower[-1] if lower else shard, axis, pairs))  41.8 us
    ppermute x7, starting transfers between devices, extended(): before = lax.ppermute(last, axis, up)  15.3 us
    ppermute x7, waiting for transfers between devices, extended(): after = lax.ppermute(leading, axis, down)  10.6 us
    ppermute x3, starting transfers between devices, collect(): upper.append(lax.ppermute(upper[-1] if upper else shard, axis, back))  10.2 us
    unnamed x57, local copies, waits for them, and re-layouts  9.92 us
    ppermute x7, starting transfers between devices, extended(): after = lax.ppermute(leading, axis, down)  9.02 us
    dot_general x5, matrix products, tap_product(): jnp.dot(flattened, weight.reshape(channels, weight.shape[-1]), preferred_...  6.75 us
  transfers between devices with their start and end apart: 23, of which 9 were waited for; matrix products, arithmetic and copies ran while one was open for 12% of the time, Pallas kernels for 0%

profile of v1, /device:TPU:0, one launch (start us, length us, event | category | flops | bytes accessed | tf_op | source)
XLA Modules:
  0.0 175.4 jit_solution(29686202189091227)
XLA Ops:
  7.3 3.0 %collective-permute-start.12 = (bf16[9,48,384]{2,1,0:T(8,128)(2,1)}, bf16[9,48,384]{2,1,0:T(8,128)(2,1)}, u32[]{:S(2)}, u32[]{:S(2)}) collective-permute-start(bf16[9,48,384]{2,1,0:T(8,128)(2,1)} %param.14), channel_id=1, source_target_pairs={{0,2},{2,4},{4,6},{6,8},{8,10},{10,12},{12,14},{14,0},{1,3},{3,5},... | collective-permute-start | bytes 995336 | tf_op jit(solution)/shard_map/ppermute | solution.py:24
  10.3 3.1 %collective-permute-start.16 = (bf16[9,48,384]{2,1,0:T(8,128)(2,1)}, bf16[9,48,384]{2,1,0:T(8,128)(2,1)S(1)}, u32[]{:S(2)}, u32[]{:S(2)}) collective-permute-start(bf16[9,48,384]{2,1,0:T(8,128)(2,1)} %param.14), channel_id=1, source_target_pairs={{2,0},{4,2},{6,4},{8,6},{10,8},{12,10},{14,12},{0,14},{3,1},{5,3},... | collective-permute-start | bytes 995336 | tf_op jit(solution)/shard_map/ppermute | solution.py:26
  14.2 1.3 collective-permute-start
  15.5 1.3 collective-permute-start.1
  17.7 42.9 %all_gather.10 = bf16[9,128,384]{2,1,0:T(8,128)(2,1)S(1)} all-gather(bf16[9,16,384]{2,1,0:T(8,128)(2,1)} %param.12), channel_id=1, replica_groups=mesh['segment'=2,'rows'=8,'cols'=2] {'rows'}, dimensions={1}, use_global_device_ids=true | all-gather | bytes 995328 | tf_op jit(solution)/shard_map/all_gather | solution.py:159
  60.7 1.3 collective-permute-start.2
  62.0 1.3 collective-permute-start.3
  63.3 1.7 collective-permute-done.3
  65.8 16.5 %collective-permute-done.13 = bf16[9,48,384]{2,1,0:T(8,128)(2,1)S(1)} collective-permute-done((bf16[9,48,384]{2,1,0:T(8,128)(2,1)}, bf16[9,48,384]{2,1,0:T(8,128)(2,1)S(1)}, u32[]{:S(2)}, u32[]{:S(2)}) %collective-permute-start.13) | collective-permute-done | bytes 331808 | tf_op jit(solution)/shard_map/ppermute | solution.py:24
  82.5 4.8 %collective-permute-start.17 = (bf16[9,48,384]{2,1,0:T(8,128)(2,1)S(1)}, bf16[9,48,384]{2,1,0:T(8,128)(2,1)}, u32[]{:S(2)}, u32[]{:S(2)}) collective-permute-start(bf16[9,48,384]{2,1,0:T(8,128)(2,1)S(1)} %collective-permute-done.16), channel_id=1, source_target_pairs={{2,0},{4,2},{6,4},{8,6},{10,8},{12,10},{14,12},{0,14},{3,1},{5,3},... | collective-permute-start | bytes 995336 | tf_op jit(solution)/shard_map/ppermute | solution.py:26
  87.2 13.2 %collective-permute-done.14 = bf16[9,48,384]{2,1,0:T(8,128)(2,1)S(1)} collective-permute-done((bf16[9,48,384]{2,1,0:T(8,128)(2,1)S(1)}, bf16[9,48,384]{2,1,0:T(8,128)(2,1)S(1)}, u32[]{:S(2)}, u32[]{:S(2)}) %collective-permute-start.14) | collective-permute-done | bytes 331808 | tf_op jit(solution)/shard_map/ppermute | solution.py:24
  100.4 2.5 %collective-permute-start.15 = (bf16[9,48,384]{2,1,0:T(8,128)(2,1)S(1)}, bf16[9,48,384]{2,1,0:T(8,128)(2,1)S(1)}, u32[]{:S(2)}, u32[]{:S(2)}) collective-permute-start(bf16[9,48,384]{2,1,0:T(8,128)(2,1)S(1)} %collective-permute-done.14), channel_id=1, source_target_pairs={{0,2},{2,4},{4,6},{6,8},{8,10},{10,12},{12,14},{14,0},{1,3},{3,5},... | collective-permute-start | bytes 995336 | tf_op jit(solution)/shard_map/ppermute | solution.py:24
  103.0 2.3 %collective-permute-start.18 = (bf16[9,48,384]{2,1,0:T(8,128)(2,1)}, bf16[9,48,384]{2,1,0:T(8,128)(2,1)}, u32[]{:S(2)}, u32[]{:S(2)}) collective-permute-start(bf16[9,48,384]{2,1,0:T(8,128)(2,1)} %collective-permute-done.17), channel_id=1, source_target_pairs={{2,0},{4,2},{6,4},{8,6},{10,8},{12,10},{14,12},{0,14},{3,1},{5,3},... | collective-permute-start | bytes 995336 | tf_op jit(solution)/shard_map/ppermute | solution.py:26
  105.2 12.0 %collective-permute-done.15 = bf16[9,48,384]{2,1,0:T(8,128)(2,1)S(1)} collective-permute-done((bf16[9,48,384]{2,1,0:T(8,128)(2,1)S(1)}, bf16[9,48,384]{2,1,0:T(8,128)(2,1)S(1)}, u32[]{:S(2)}, u32[]{:S(2)}) %collective-permute-start.15) | collective-permute-done | bytes 331808 | tf_op jit(solution)/shard_map/ppermute | solution.py:24
  119.6 1.7 bitcast_dynamic-update-slice_fusion.4
  121.3 2.3 %convolution_add_fusion.1 = f32[2,64,512]{2,1,0:T(8,128)S(1)} fusion(bf16[2,64,2304]{2,1,0:T(8,128)(2,1)S(1)} %constant_dynamic-update-slice_fusion, bf16[2304,512,1]{1,0,2:T(8,128)(2,1)} %bitcast.49, f32[512]{0:T(512)S(1)} %copy-done.7), kind=kOutput, calls=%fused_computation.2 | convolution fusion | flops 302055424 | bytes 3213312 | tf_op jit(solution)/shard_map/cond/branch_1_fun/dot_general | solution.py:64
  123.7 3.7 %collective-permute-start.4 = (bf16[1,64,256]{2,1,0:T(8,128)(2,1)S(1)}, bf16[1,64,256]{2,1,0:T(8,128)(2,1)S(1)}, u32[]{:S(2)}, u32[]{:S(2)}) collective-permute-start(bf16[1,64,256]{2,1,0:T(8,128)(2,1)S(1)} %get-tuple-element.19), channel_id=1, source_target_pairs={{0,2},{2,4},{4,6},{6,8},{8,10},{10,12},{12,14},{1,3},{3,5},{5,7},{... | collective-permute-start | bytes 98312 | tf_op jit(solution)/shard_map/ppermute | solution.py:40
  127.4 1.3 collective-permute-start.5
  129.7 4.3 %collective-permute-done.5 = bf16[1,64,256]{2,1,0:T(8,128)(2,1)S(1)} collective-permute-done((bf16[1,64,256]{2,1,0:T(8,128)(2,1)S(1)}, bf16[1,64,256]{2,1,0:T(8,128)(2,1)S(1)}, u32[]{:S(2)}, u32[]{:S(2)}) %collective-permute-start.5) | collective-permute-done | bytes 32800 | tf_op jit(solution)/shard_map/ppermute | solution.py:41
  134.0 1.3 collective-permute-start.6
  135.3 1.3 collective-permute-start.7
  136.6 1.8 %bitcast_dynamic-update-slice_fusion.2 = bf16[8,9,48,384]{3,2,1,0:T(8,128)(2,1)} fusion(bf16[8,9,48,384]{3,2,1,0:T(8,128)(2,1)} %bitcast_dynamic-update-slice_fusion.3, bf16[9,48,384]{2,1,0:T(8,128)(2,1)} %copy-done.5), kind=kLoop, calls=%fused_computation.16 | loop fusion | bytes 663552
  139.3 3.0 %collective-permute-start.8 = (bf16[2,16,128]{2,1,0:T(8,128)(2,1)S(1)}, bf16[2,16,128]{2,1,0:T(8,128)(2,1)S(1)}, u32[]{:S(2)}, u32[]{:S(2)}) collective-permute-start(bf16[2,16,128]{2,1,0:T(8,128)(2,1)S(1)} %get-tuple-element.22), channel_id=1, source_target_pairs={{0,1},{2,3},{4,5},{6,7},{8,9},{10,11},{12,13},{14,15},{16,17},{18,... | collective-permute-start | bytes 24584 | tf_op jit(solution)/shard_map/ppermute | solution.py:40
  142.3 1.8 %bitcast_dynamic-update-slice_fusion.1 = bf16[8,9,48,384]{3,2,1,0:T(8,128)(2,1)} fusion(bf16[8,9,48,384]{3,2,1,0:T(8,128)(2,1)} %bitcast_dynamic-update-slice_fusion.2, bf16[9,48,384]{2,1,0:T(8,128)(2,1)} %collective-permute-done.17), kind=kLoop, calls=%fused_computation.15 | loop fusion | bytes 663552
  145.4 1.7 collective-permute-done.9
  148.1 2.7 %collective-permute-start.10 = (bf16[2,32,384]{2,1,0:T(8,128)(2,1)}, bf16[2,32,384]{2,1,0:T(8,128)(2,1)}, u32[]{:S(2)}, u32[]{:S(2)}) collective-permute-start(bf16[2,32,384]{2,1,0:T(8,128)(2,1)} %get-tuple-element.18), channel_id=1, source_target_pairs={{0,1},{2,3},{4,5},{6,7},{8,9},{10,11},{12,13},{14,15},{16,17},{18,... | collective-permute-start | bytes 147464 | tf_op jit(solution)/shard_map/ppermute | solution.py:40
  150.8 1.7 bitcast_dynamic-update-slice_fusion
  152.6 2.9 %gather_fusion = bf16[8,9,48,384]{3,2,1,0:T(8,128)(2,1)S(1)} fusion(bf16[8,9,48,384]{3,2,1,0:T(8,128)(2,1)} %bitcast_dynamic-update-slice_fusion, s32[1024]{0:T(1024)S(1)} %pad_clamp_fusion), kind=kCustom, calls=%fused_computation | custom fusion | bytes 5308448 | tf_op jit(solution)/shard_map/gather | solution.py:29
  160.1 2.1 %collective-permute-start.19 = (bf16[2,64,384]{2,1,0:T(8,128)(2,1)S(1)}, bf16[2,64,384]{2,1,0:T(8,128)(2,1)S(1)}, u32[]{:S(2)}, u32[]{:S(2)}) collective-permute-start(bf16[2,64,384]{2,1,0:T(8,128)(2,1)S(1)} %fusion.5), channel_id=1, source_target_pairs={{0,1},{2,3},{4,5},{6,7},{8,9},{10,11},{12,13},{14,15},{16,17},{18,... | collective-permute-start | bytes 294920 | tf_op jit(solution)/shard_map/ppermute | solution.py:40
  162.2 1.3 collective-permute-start.20
  163.6 1.8 %collective-permute-done.20 = bf16[2,64,384]{2,1,0:T(8,128)(2,1)S(1)} collective-permute-done((bf16[2,64,384]{2,1,0:T(8,128)(2,1)S(1)}, bf16[2,64,384]{2,1,0:T(8,128)(2,1)S(1)}, u32[]{:S(2)}, u32[]{:S(2)}) %collective-permute-start.20) | collective-permute-done | bytes 98336 | tf_op jit(solution)/shard_map/ppermute | solution.py:41
  165.5 3.0 %fusion.7 = bf16[1,2,64,384]{3,2,1,0:T(8,128)(2,1)} fusion(bf16[2,64,3456]{2,1,0:T(8,128)(2,1)S(1)} %constant_dynamic-update-slice_fusion.34, bf16[3456,384,1]{1,0,2:T(8,128)(2,1)} %bitcast.52, bf16[2,64,384]{2,1,0:T(8,128)(2,1)S(1)} %fusion.5, f32[384]{0:T(512)S(1)} %copy-done.8), kind=kOutput, calls=%fused_computation.13 | convolution fusion | flops 339984384 | bytes 3737088 | tf_op jit(solution)/shard_map/cond/branch_1_fun/dot_general | solution.py:64
  (109 shorter events, 14.4 us)
Async XLA Ops:
  6.5 114.8 %all-gather.3.cloned.1.call-start = ((), (), s32[]{:S(2)}) async-start(), calls=%async_computation | async-start | bytes 2654208 | tf_op jit(solution)/shard_map/all_gather | solution.py:158
  7.3 158.3 %all-gather.5.cloned.1.call-start = ((), (), s32[]{:S(2)}) async-start(), calls=%async_computation.1 | async-start | bytes 2985984 | tf_op jit(solution)/shard_map/all_gather | solution.py:161
  7.3 57.9 %collective-permute-start.12 = (bf16[9,48,384]{2,1,0:T(8,128)(2,1)}, bf16[9,48,384]{2,1,0:T(8,128)(2,1)}, u32[]{:S(2)}, u32[]{:S(2)}) collective-permute-start(bf16[9,48,384]{2,1,0:T(8,128)(2,1)} %param.14), channel_id=1, source_target_pairs={{0,2},{2,4},{4,6},{6,8},{8,10},{10,12},{12,14},{14,0},{1,3},{3,5},... | collective-permute-start | bytes 995336 | tf_op jit(solution)/shard_map/ppermute | solution.py:24
  10.3 72.1 %collective-permute-start.16 = (bf16[9,48,384]{2,1,0:T(8,128)(2,1)}, bf16[9,48,384]{2,1,0:T(8,128)(2,1)S(1)}, u32[]{:S(2)}, u32[]{:S(2)}) collective-permute-start(bf16[9,48,384]{2,1,0:T(8,128)(2,1)} %param.14), channel_id=1, source_target_pairs={{2,0},{4,2},{6,4},{8,6},{10,8},{12,10},{14,12},{0,14},{3,1},{5,3},... | collective-permute-start | bytes 995336 | tf_op jit(solution)/shard_map/ppermute | solution.py:26
  14.2 46.4 %collective-permute-start = (bf16[1,64,256]{2,1,0:T(8,128)(2,1)S(1)}, bf16[1,64,256]{2,1,0:T(8,128)(2,1)S(1)}, u32[]{:S(2)}, u32[]{:S(2)}) collective-permute-start(bf16[1,64,256]{2,1,0:T(8,128)(2,1)S(1)} %get-tuple-element.23), channel_id=1, source_target_pairs={{0,2},{2,4},{4,6},{6,8},{8,10},{10,12},{12,14},{1,3},{3,5},{5,7},{... | collective-permute-start | bytes 98312 | tf_op jit(solution)/shard_map/ppermute | solution.py:40
  15.5 45.1 %collective-permute-start.1 = (bf16[1,64,256]{2,1,0:T(8,128)(2,1)S(1)}, bf16[1,64,256]{2,1,0:T(8,128)(2,1)S(1)}, u32[]{:S(2)}, u32[]{:S(2)}) collective-permute-start(bf16[1,64,256]{2,1,0:T(8,128)(2,1)S(1)} %get-tuple-element.24), channel_id=1, source_target_pairs={{2,0},{4,2},{6,4},{8,6},{10,8},{12,10},{14,12},{3,1},{5,3},{7,5},{... | collective-permute-start | bytes 98312 | tf_op jit(solution)/shard_map/ppermute | solution.py:41
  17.7 103.6 %copy-start.7 = (f32[512]{0:T(512)S(1)}, f32[512]{0:T(512)}, u32[]{:S(2)}) copy-start(f32[512]{0:T(512)} %param.11) | copy-start | bytes 6148
  60.7 2.6 %collective-permute-start.2 = (bf16[4,1,256]{2,1,0:T(2,128)(2,1)S(1)}, bf16[4,1,256]{2,1,0:T(2,128)(2,1)S(1)}, u32[]{:S(2)}, u32[]{:S(2)}) collective-permute-start(bf16[4,1,256]{2,1,0:T(2,128)(2,1)S(1)} %get-tuple-element.16), channel_id=1, source_target_pairs={{0,1},{2,3},{4,5},{6,7},{8,9},{10,11},{12,13},{14,15},{16,17},{18,... | collective-permute-start | bytes 6152 | tf_op jit(solution)/shard_map/ppermute | solution.py:40
  62.0 3.1 %collective-permute-start.3 = (bf16[4,1,256]{2,1,0:T(2,128)(2,1)S(1)}, bf16[4,1,256]{2,1,0:T(2,128)(2,1)S(1)}, u32[]{:S(2)}, u32[]{:S(2)}) collective-permute-start(bf16[4,1,256]{2,1,0:T(2,128)(2,1)S(1)} %get-tuple-element.15), channel_id=1, source_target_pairs={{1,0},{3,2},{5,4},{7,6},{9,8},{11,10},{13,12},{15,14},{17,16},{19,... | collective-permute-start | bytes 6152 | tf_op jit(solution)/shard_map/ppermute | solution.py:41
  65.2 17.2 %collective-permute-start.13 = (bf16[9,48,384]{2,1,0:T(8,128)(2,1)}, bf16[9,48,384]{2,1,0:T(8,128)(2,1)S(1)}, u32[]{:S(2)}, u32[]{:S(2)}) collective-permute-start(bf16[9,48,384]{2,1,0:T(8,128)(2,1)} %collective-permute-done.12), channel_id=1, source_target_pairs={{0,2},{2,4},{4,6},{6,8},{8,10},{10,12},{12,14},{14,0},{1,3},{3,5},... | collective-permute-start | bytes 995336 | tf_op jit(solution)/shard_map/ppermute | solution.py:24
  82.4 18.0 %collective-permute-start.14 = (bf16[9,48,384]{2,1,0:T(8,128)(2,1)S(1)}, bf16[9,48,384]{2,1,0:T(8,128)(2,1)S(1)}, u32[]{:S(2)}, u32[]{:S(2)}) collective-permute-start(bf16[9,48,384]{2,1,0:T(8,128)(2,1)S(1)} %collective-permute-done.13), channel_id=1, source_target_pairs={{0,2},{2,4},{4,6},{6,8},{8,10},{10,12},{12,14},{14,0},{1,3},{3,5},... | collective-permute-start | bytes 995336 | tf_op jit(solution)/shard_map/ppermute | solution.py:24
  82.4 35.6 %copy-start.5 = (bf16[9,48,384]{2,1,0:T(8,128)(2,1)}, bf16[9,48,384]{2,1,0:T(8,128)(2,1)S(1)}, u32[]{:S(2)}) copy-start(bf16[9,48,384]{2,1,0:T(8,128)(2,1)S(1)} %collective-permute-done.16) | copy-start | bytes 995332
  82.5 20.5 %collective-permute-start.17 = (bf16[9,48,384]{2,1,0:T(8,128)(2,1)S(1)}, bf16[9,48,384]{2,1,0:T(8,128)(2,1)}, u32[]{:S(2)}, u32[]{:S(2)}) collective-permute-start(bf16[9,48,384]{2,1,0:T(8,128)(2,1)S(1)} %collective-permute-done.16), channel_id=1, source_target_pairs={{2,0},{4,2},{6,4},{8,6},{10,8},{12,10},{14,12},{0,14},{3,1},{5,3},... | collective-permute-start | bytes 995336 | tf_op jit(solution)/shard_map/ppermute | solution.py:26
  100.4 16.8 %collective-permute-start.15 = (bf16[9,48,384]{2,1,0:T(8,128)(2,1)S(1)}, bf16[9,48,384]{2,1,0:T(8,128)(2,1)S(1)}, u32[]{:S(2)}, u32[]{:S(2)}) collective-permute-start(bf16[9,48,384]{2,1,0:T(8,128)(2,1)S(1)} %collective-permute-done.14), channel_id=1, source_target_pairs={{0,2},{2,4},{4,6},{6,8},{8,10},{10,12},{12,14},{14,0},{1,3},{3,5},... | collective-permute-start | bytes 995336 | tf_op jit(solution)/shard_map/ppermute | solution.py:24
  103.0 47.9 %collective-permute-start.18 = (bf16[9,48,384]{2,1,0:T(8,128)(2,1)}, bf16[9,48,384]{2,1,0:T(8,128)(2,1)}, u32[]{:S(2)}, u32[]{:S(2)}) collective-permute-start(bf16[9,48,384]{2,1,0:T(8,128)(2,1)} %collective-permute-done.17), channel_id=1, source_target_pairs={{2,0},{4,2},{6,4},{8,6},{10,8},{12,10},{14,12},{0,14},{3,1},{5,3},... | collective-permute-start | bytes 995336 | tf_op jit(solution)/shard_map/ppermute | solution.py:26
  118.8 9.9 %copy-start.4 = (bf16[9,48,384]{2,1,0:T(8,128)(2,1)S(1)}, bf16[9,48,384]{2,1,0:T(8,128)(2,1)}, u32[]{:S(2)}) copy-start(bf16[9,48,384]{2,1,0:T(8,128)(2,1)} %param.14) | copy-start | bytes 995332
  121.3 17.4 %copy-start = (bf16[9,256,512]{2,1,0:T(8,128)(2,1)S(1)}, bf16[9,256,512]{2,1,0:T(8,128)(2,1)}, u32[]{:S(2)}) copy-start(bf16[9,256,512]{2,1,0:T(8,128)(2,1)} %all-gather.3.cloned.1.call-done) | copy-start | bytes 7077892
  123.7 6.0 %collective-permute-start.4 = (bf16[1,64,256]{2,1,0:T(8,128)(2,1)S(1)}, bf16[1,64,256]{2,1,0:T(8,128)(2,1)S(1)}, u32[]{:S(2)}, u32[]{:S(2)}) collective-permute-start(bf16[1,64,256]{2,1,0:T(8,128)(2,1)S(1)} %get-tuple-element.19), channel_id=1, source_target_pairs={{0,2},{2,4},{4,6},{6,8},{8,10},{10,12},{12,14},{1,3},{3,5},{5,7},{... | collective-permute-start | bytes 98312 | tf_op jit(solution)/shard_map/ppermute | solution.py:40
  127.4 6.6 %collective-permute-start.5 = (bf16[1,64,256]{2,1,0:T(8,128)(2,1)S(1)}, bf16[1,64,256]{2,1,0:T(8,128)(2,1)S(1)}, u32[]{:S(2)}, u32[]{:S(2)}) collective-permute-start(bf16[1,64,256]{2,1,0:T(8,128)(2,1)S(1)} %get-tuple-element.20), channel_id=1, source_target_pairs={{2,0},{4,2},{6,4},{8,6},{10,8},{12,10},{14,12},{3,1},{5,3},{7,5},{... | collective-permute-start | bytes 98312 | tf_op jit(solution)/shard_map/ppermute | solution.py:41
  134.0 4.4 %collective-permute-start.6 = (bf16[4,1,256]{2,1,0:T(2,128)(2,1)S(1)}, bf16[4,1,256]{2,1,0:T(2,128)(2,1)S(1)}, u32[]{:S(2)}, u32[]{:S(2)}) collective-permute-start(bf16[4,1,256]{2,1,0:T(2,128)(2,1)S(1)} %get-tuple-element.10), channel_id=1, source_target_pairs={{0,1},{2,3},{4,5},{6,7},{8,9},{10,11},{12,13},{14,15},{16,17},{18,... | collective-permute-start | bytes 6152 | tf_op jit(solution)/shard_map/ppermute | solution.py:40
  135.3 3.1 %collective-permute-start.7 = (bf16[4,1,256]{2,1,0:T(2,128)(2,1)S(1)}, bf16[4,1,256]{2,1,0:T(2,128)(2,1)S(1)}, u32[]{:S(2)}, u32[]{:S(2)}) collective-permute-start(bf16[4,1,256]{2,1,0:T(2,128)(2,1)S(1)} %get-tuple-element.9), channel_id=1, source_target_pairs={{1,0},{3,2},{5,4},{7,6},{9,8},{11,10},{13,12},{15,14},{17,16},{19,... | collective-permute-start | bytes 6152 | tf_op jit(solution)/shard_map/ppermute | solution.py:41
  138.5 8.6 %copy-start.10 = (f32[384]{0:T(512)S(1)}, f32[384]{0:T(512)}, u32[]{:S(2)}) copy-start(f32[384]{0:T(512)} %param.13) | copy-start | bytes 4612
  139.3 6.1 %collective-permute-start.8 = (bf16[2,16,128]{2,1,0:T(8,128)(2,1)S(1)}, bf16[2,16,128]{2,1,0:T(8,128)(2,1)S(1)}, u32[]{:S(2)}, u32[]{:S(2)}) collective-permute-start(bf16[2,16,128]{2,1,0:T(8,128)(2,1)S(1)} %get-tuple-element.22), channel_id=1, source_target_pairs={{0,1},{2,3},{4,5},{6,7},{8,9},{10,11},{12,13},{14,15},{16,17},{18,... | collective-permute-start | bytes 24584 | tf_op jit(solution)/shard_map/ppermute | solution.py:40
  144.0 3.1 %collective-permute-start.9 = (bf16[2,16,128]{2,1,0:T(8,128)(2,1)S(1)}, bf16[2,16,128]{2,1,0:T(8,128)(2,1)S(1)}, u32[]{:S(2)}, u32[]{:S(2)}) collective-permute-start(bf16[2,16,128]{2,1,0:T(8,128)(2,1)S(1)} %get-tuple-element.21), channel_id=1, source_target_pairs={{1,0},{3,2},{5,4},{7,6},{9,8},{11,10},{13,12},{15,14},{17,16},{19,... | collective-permute-start | bytes 24584 | tf_op jit(solution)/shard_map/ppermute | solution.py:41
  147.5 3.4 %copy-start.1 = (bf16[2,64,384]{2,1,0:T(8,128)(2,1)}, bf16[2,64,384]{2,1,0:T(8,128)(2,1)S(1)}, u32[]{:S(2)}) copy-start(bf16[2,64,384]{2,1,0:T(8,128)(2,1)S(1)} %fusion.4) | copy-start | bytes 294916
  148.1 9.4 %collective-permute-start.10 = (bf16[2,32,384]{2,1,0:T(8,128)(2,1)}, bf16[2,32,384]{2,1,0:T(8,128)(2,1)}, u32[]{:S(2)}, u32[]{:S(2)}) collective-permute-start(bf16[2,32,384]{2,1,0:T(8,128)(2,1)} %get-tuple-element.18), channel_id=1, source_target_pairs={{0,1},{2,3},{4,5},{6,7},{8,9},{10,11},{12,13},{14,15},{16,17},{18,... | collective-permute-start | bytes 147464 | tf_op jit(solution)/shard_map/ppermute | solution.py:40
  155.5 4.0 %copy-start.9 = (f32[384]{0:T(512)S(1)}, f32[384]{0:T(512)}, u32[]{:S(2)}) copy-start(f32[384]{0:T(512)} %param.15) | copy-start | bytes 4612
  156.2 3.1 %collective-permute-start.11 = (bf16[2,32,384]{2,1,0:T(8,128)(2,1)S(1)}, bf16[2,32,384]{2,1,0:T(8,128)(2,1)S(1)}, u32[]{:S(2)}, u32[]{:S(2)}) collective-permute-start(bf16[2,32,384]{2,1,0:T(8,128)(2,1)S(1)} %copy-done.6), channel_id=1, source_target_pairs={{1,0},{3,2},{5,4},{7,6},{9,8},{11,10},{13,12},{15,14},{17,16},{19,... | collective-permute-start | bytes 147464 | tf_op jit(solution)/shard_map/ppermute | solution.py:41
  159.4 2.8 %copy-start.3 = (bf16[2,64,3456]{2,1,0:T(8,128)(2,1)S(1)}, bf16[2,64,3456]{2,1,0:T(8,128)(2,1)}, u32[]{:S(2)}) copy-start(bf16[2,64,3456]{2,1,0:T(8,128)(2,1)} %constant_dynamic-update-slice_fusion.40) | copy-start | bytes 2654212
  159.4 6.1 %copy-start.8 = (f32[384]{0:T(512)S(1)}, f32[384]{0:T(512)}, u32[]{:S(2)}) copy-start(f32[384]{0:T(512)} %param.17) | copy-start | bytes 4612
  160.1 3.4 %collective-permute-start.19 = (bf16[2,64,384]{2,1,0:T(8,128)(2,1)S(1)}, bf16[2,64,384]{2,1,0:T(8,128)(2,1)S(1)}, u32[]{:S(2)}, u32[]{:S(2)}) collective-permute-start(bf16[2,64,384]{2,1,0:T(8,128)(2,1)S(1)} %fusion.5), channel_id=1, source_target_pairs={{0,1},{2,3},{4,5},{6,7},{8,9},{10,11},{12,13},{14,15},{16,17},{18,... | collective-permute-start | bytes 294920 | tf_op jit(solution)/shard_map/ppermute | solution.py:40
  162.2 3.2 %collective-permute-start.20 = (bf16[2,64,384]{2,1,0:T(8,128)(2,1)S(1)}, bf16[2,64,384]{2,1,0:T(8,128)(2,1)S(1)}, u32[]{:S(2)}, u32[]{:S(2)}) collective-permute-start(bf16[2,64,384]{2,1,0:T(8,128)(2,1)S(1)} %fusion.5), channel_id=1, source_target_pairs={{1,0},{3,2},{5,4},{7,6},{9,8},{11,10},{13,12},{15,14},{17,16},{19,... | collective-permute-start | bytes 294920 | tf_op jit(solution)/shard_map/ppermute | solution.py:41
  (2 other events, 2.9 us)
Sparse Core Ops, SparseCore 0:
  9.5 64.5 all-gather.2
  76.3 70.8 all-gather.4
